TPU v7x, 256 devices: a whole 4x4x8 slice. The times are simulated.
256 devices in a mesh: tm: 8 (over y, core), head: 32 (over z, x).
Axes of the slice: x: 4, y: 4, z: 8, core: 2. Of those that a mesh axis runs over, the one named last changes fastest.
Arguments:
- tokens: bfloat16 [4096, 5120], P('tm'), may hold values from -24 to 24
- w_query: bfloat16 [5120, 4096], P(None, 'head'), may hold values from -0.078125 to 0.078125
- w_key: bfloat16 [5120, 4096], P(None, 'head'), may hold values from -0.078125 to 0.078125
- w_value: bfloat16 [5120, 4096], P(None, 'head'), may hold values from -0.078125 to 0.078125
- w_out: bfloat16 [4096, 5120], P('head'), may hold values from -0.09375 to 0.09375
- out_grad: bfloat16 [4096, 5120], P('tm'), may hold values from -6 to 6
- frame_lists: int32 [8, 8], replicated, may hold values from 0 to 1, as said below
Outputs:
- token_grad: bfloat16 [4096, 5120], P(('tm', 'head'))
- query_grad: bfloat16 [5120, 4096], P('tm', 'head')
- key_grad: bfloat16 [5120, 4096], P('tm', 'head')
- value_grad: bfloat16 [5120, 4096], P('tm', 'head')
- out_weight_grad: bfloat16 [4096, 5120], P('head', 'tm')
Inputs may be any that keep to these rules, and one draw needn't show every extreme that they name: `frame_lists`: entries with j >= i are 0; entry (i, i - 1) is 1 for every group i > 0.
All inputs are finite; a program needn't handle non-finite values.
Results may differ from a plain program's by a relative error of at most 0.02.
The roundings to bfloat16 on the way count: a program that leaves them out, or rounds other values in their place, can miss the bound.
Values may be sent and summed in bfloat16 or wider, within the bound.
A program may use at most 128 MiB of HBM per device.

v0:
```python
import jax
import jax.numpy as jnp
from jax import lax
from jax.sharding import PartitionSpec as P


def contract_rows(left, right):
    return lax.dot_general(
        left, right, (((0,), (0,)), ((), ())), preferred_element_type=jnp.float32
    )


def contract_cols(left, right):
    return lax.dot_general(
        left, right, (((1,), (1,)), ((), ())), preferred_element_type=jnp.float32
    )


def local(tokens, w_query, w_key, w_value, w_out, out_grad, frame_lists):
    width = w_query.shape[1]
    scale = 1.0 / width**0.5
    rows = tokens.shape[0]
    groups = lax.axis_size("tm")
    mine = lax.axis_index("tm")
    query = jnp.dot(tokens, w_query, preferred_element_type=jnp.float32).astype(jnp.bfloat16)
    keys = jnp.dot(tokens, w_key, preferred_element_type=jnp.float32).astype(jnp.bfloat16)
    values = jnp.dot(tokens, w_value, preferred_element_type=jnp.float32).astype(jnp.bfloat16)
    d_attn = contract_cols(out_grad, w_out).astype(jnp.bfloat16)
    my_list = lax.dynamic_slice_in_dim(frame_lists, mine, 1, 0)[0]
    key_all, value_all = (
        lax.all_gather(keys, "tm", axis=0, tiled=True),
        lax.all_gather(values, "tm", axis=0, tiled=True),
    )
    order = jnp.arange(groups, dtype=jnp.int32)
    allowed = (order == mine) | (my_list == 1) & (order < mine)
    key_mask = jnp.repeat(allowed, rows)[None, :]
    scores = contract_cols(query, key_all) * scale
    scores = jnp.where(key_mask, scores, jnp.float32(-1e30))
    top = jnp.max(scores, axis=1, keepdims=True)
    expd = jnp.exp(scores - top)
    probs = expd / jnp.sum(expd, axis=1, keepdims=True)
    probs_b = probs.astype(jnp.bfloat16)
    attn = jnp.dot(probs_b, value_all, preferred_element_type=jnp.float32).astype(jnp.bfloat16)
    dprobs = contract_cols(d_attn, value_all)
    delta = jnp.sum(probs * dprobs, axis=1, keepdims=True)
    dscore = (probs * (dprobs - delta) * scale).astype(jnp.bfloat16)
    dquery = jnp.dot(dscore, key_all, preferred_element_type=jnp.float32).astype(jnp.bfloat16)
    cache_terms = jnp.concatenate(
        [contract_rows(dscore, query), contract_rows(probs_b, d_attn)], axis=1
    )
    summed = lax.psum_scatter(
        cache_terms.astype(jnp.bfloat16), "tm", scatter_dimension=0, tiled=True
    ).astype(jnp.float32)
    dkey = summed[:, :width].astype(jnp.bfloat16)
    dvalue = summed[:, width:].astype(jnp.bfloat16)
    weights_sum = lax.psum_scatter(
        jnp.concatenate(
            [
                contract_rows(tokens, dquery),
                contract_rows(tokens, dkey),
                contract_rows(tokens, dvalue),
                contract_rows(out_grad, attn),
            ],
            axis=1,
        ).astype(jnp.bfloat16),
        "tm",
        scatter_dimension=0,
        tiled=True,
    ).astype(jnp.float32)
    query_grad = weights_sum[:, :width].astype(jnp.bfloat16)
    key_grad = weights_sum[:, width : 2 * width].astype(jnp.bfloat16)
    value_grad = weights_sum[:, 2 * width : 3 * width].astype(jnp.bfloat16)
    out_weight_grad = weights_sum[:, 3 * width :].T.astype(jnp.bfloat16)
    token_grad = lax.psum_scatter(
        (
            contract_cols(dquery, w_query)
            + contract_cols(dkey, w_key)
            + contract_cols(dvalue, w_value)
        ).astype(jnp.bfloat16),
        "head",
        scatter_dimension=0,
        tiled=True,
    )
    return (token_grad, query_grad, key_grad, value_grad, out_weight_grad)


def solution(mesh):
    in_specs = (
        P("tm", None),
        P(None, "head"),
        P(None, "head"),
        P(None, "head"),
        P("head", None),
        P("tm", None),
        P(),
    )
    out_specs = (
        P(("tm", "head"), None),
        P("tm", "head"),
        P("tm", "head"),
        P("tm", "head"),
        P("head", "tm"),
    )
    return jax.shard_map(local, mesh=mesh, in_specs=in_specs, out_specs=out_specs, check_vma=False)
```

profile of v0, /device:TPU:8, one launch (start us, length us, event | category | flops | bytes accessed | tf_op | source)
XLA Modules:
  0.0 424.9 jit_solution(9849481897770291235)
XLA Ops:
  7.2 5.2 %convolution_convert_fusion.9 = bf16[512,128]{1,0:T(8,128)(2,1)} fusion(bf16[512,5120]{1,0:T(8,128)(2,1)} %param.7, bf16[5120,128]{1,0:T(8,128)(2,1)} %param.9), kind=kOutput, calls=%fused_computation.26 | convolution fusion | flops 671154176 | bytes 6684672 | tf_op jit(solution)/shard_map/dot_general | solution.py:26
  12.5 4.7 %convolution_convert_fusion.7 = bf16[512,128]{1,0:T(8,128)(2,1)} fusion(bf16[512,5120]{1,0:T(8,128)(2,1)} %param.7, bf16[5120,128]{1,0:T(8,128)(2,1)S(1)} %copy-done.7), kind=kOutput, calls=%fused_computation.24 | convolution fusion | flops 671154176 | bytes 6684672 | tf_op jit(solution)/shard_map/dot_general | solution.py:27
  18.1 4.0 convolution_convert_fusion.10
  22.2 4.0 convolution_convert_fusion.8
  26.2 13.5 %all-gather.3.cloned.1.call-done = bf16[4096,128]{1,0:T(8,128)(2,1)} async-done(((bf16[512,128]{1,0:T(8,128)(2,1)}), bf16[4096,128]{1,0:T(8,128)(2,1)}) %all-gather.3.cloned.1.call-update) | async-done | bytes 1048592 | tf_op jit(solution)/shard_map/all_gather | solution.py:31
  39.7 2.7 fusion
  42.5 3.2 copy-done.2
  45.7 2.2 fusion.2
  47.9 20.2 %all-gather.5.cloned.1.call-done = bf16[4096,128]{1,0:T(8,128)(2,1)} async-done(((bf16[512,128]{1,0:T(8,128)(2,1)}), bf16[4096,128]{1,0:T(8,128)(2,1)}) %all-gather.5.cloned.1.call-update) | async-done | bytes 1048592 | tf_op jit(solution)/shard_map/all_gather | solution.py:32
  68.0 7.4 %multiply_reduce_fusion = (f32[512]{0:T(512)S(1)}, f32[512,4096]{1,0:T(8,128)S(1)}, f32[512,4096]{1,0:T(8,128)}) fusion(f32[512]{0:T(512)S(1)} %fusion.2, f32[512]{0:T(512)S(1)} %get-tuple-element.21, f32[512,4096]{1,0:T(8,128)} %copy-done.2, pred[4096]{0:T(1024)(128)(4,1)S(1)} %bitcast.47, bf16[512,128]{1,0:T(8,128)(2,1)S(1)} %convolution_convert_fusion.8, ...), kind=kOutput, calls=%fused_computation.2 | convolution fusion | flops 549453312 | bytes 26355712 | tf_op jit(solution)/shard_map/dot_general | solution.py:14
  76.2 2.5 copy-done.1
  78.7 8.0 %multiply_convert_fusion = bf16[512,4096]{1,0:T(8,128)(2,1)S(1)} fusion(f32[512,4096]{1,0:T(8,128)} %copy-done.1, f32[512,4096]{1,0:T(8,128)} %get-tuple-element.23, f32[512]{0:T(512)S(1)} %get-tuple-element.15), kind=kLoop, calls=%fused_computation.1 | loop fusion | flops 8388608 | bytes 20973568 | tf_op jit(solution)/shard_map/convert_element_type | solution.py:46
  91.2 3.7 convolution_convert_fusion.6
  94.9 3.4 fusion.3
  98.3 9.7 %fusion.6 = bf16[5120,128]{0,1:T(8,128)(2,1)} fusion(bf16[512,5120]{1,0:T(8,128)(2,1)} %param.12, bf16[4096,128]{1,0:T(8,128)(2,1)} %all-gather.5.cloned.1.call-done, f32[512,4096]{1,0:T(8,128)} %copy-done.1), kind=kOutput, calls=%fused_computation.15 | convolution fusion | flops 1210777600 | bytes 15990784 | tf_op jit(solution)/shard_map/dot_general | solution.py:8
  108.0 17.6 %reduce-scatter.6.cloned.1.call-done = bf16[512,256]{0,1:T(8,128)(2,1)} async-done(((bf16[4096,256]{0,1:T(8,128)(2,1)}), bf16[512,256]{0,1:T(8,128)(2,1)}) %reduce-scatter.6.cloned.1.call-update) | async-done | bytes 262160 | tf_op jit(solution)/shard_map/reduce_scatter | solution.py:51
  125.6 3.5 fusion.4
  129.1 3.4 fusion.5
  132.6 3.5 pad_maximum_fusion
  136.1 7.9 %copy.18 = bf16[5120,512]{1,0:T(8,128)(2,1)} copy(bf16[5120,512]{0,1:T(8,128)(2,1)} %pad_maximum_fusion) | data formatting | bytes 10485760
  145.6 5.5 %fusion.18 = f32[512,5120]{1,0:T(8,128)} fusion(bf16[5120,128]{1,0:T(8,128)(2,1)S(1)} %copy-done.6, bf16[512,256]{0,1:T(8,128)(2,1)S(1)} %copy-done.5), kind=kOutput, calls=%fused_computation.32 | convolution fusion | flops 671088640 | bytes 11927552 | tf_op jit(solution)/shard_map/dot_general | solution.py:14
  151.2 8.2 %add_convert_fusion = bf16[512,5120]{1,0:T(8,128)(2,1)} fusion(f32[512,5120]{1,0:T(8,128)S(1)} %fusion.23, f32[512,5120]{1,0:T(8,128)} %fusion.18, bf16[5120,128]{1,0:T(8,128)(2,1)S(1)} %copy-done.8, bf16[512,256]{0,1:T(8,128)(2,1)S(1)} %copy-done.5), kind=kOutput, calls=%fused_computation | convolution fusion | flops 678952960 | bytes 27656192 | tf_op jit(solution)/shard_map/dot_general | solution.py:14
  159.4 25.7 %reduce-scatter.10.cloned.1.call-done = bf16[640,512]{1,0:T(8,128)(2,1)} async-done(((bf16[5120,512]{1,0:T(8,128)(2,1)}), bf16[640,512]{1,0:T(8,128)(2,1)}) %reduce-scatter.10.cloned.1.call-update) | async-done | bytes 655376
  187.8 230.5 %reduce-scatter.8.cloned.1.call-done = bf16[16,5120]{1,0:T(8,128)(2,1)} async-done(((bf16[512,5120]{1,0:T(8,128)(2,1)}), bf16[16,5120]{1,0:T(8,128)(2,1)}) %reduce-scatter.8.cloned.1.call-update) | async-done | bytes 163856 | tf_op jit(solution)/shard_map/reduce_scatter | solution.py:74
  (37 shorter events, 10.6 us)
Async XLA Ops:
  7.2 11.0 %copy-start = (bf16[5120,128]{1,0:T(8,128)(2,1)S(1)}, bf16[5120,128]{1,0:T(8,128)(2,1)}, u32[]{:S(2)}) copy-start(bf16[5120,128]{1,0:T(8,128)(2,1)} %param.8) | copy-start | bytes 3932164
  7.2 5.3 %copy-start.7 = (bf16[5120,128]{1,0:T(8,128)(2,1)S(1)}, bf16[5120,128]{1,0:T(8,128)(2,1)}, u32[]{:S(2)}) copy-start(bf16[5120,128]{1,0:T(8,128)(2,1)} %param.10) | copy-start | bytes 3932164
  7.2 32.6 %all-gather.3.cloned.1.call-start = ((), (), s32[]{:S(2)}) async-start(), calls=%async_computation.3 | async-start | bytes 1179648 | tf_op jit(solution)/shard_map/all_gather | solution.py:31
  12.5 55.6 %all-gather.5.cloned.1.call-start = ((), (), s32[]{:S(2)}) async-start(), calls=%async_computation.4 | async-start | bytes 1179648 | tf_op jit(solution)/shard_map/all_gather | solution.py:32
  17.2 5.0 %copy-start.9 = (bf16[128,5120]{1,0:T(8,128)(2,1)S(1)}, bf16[128,5120]{1,0:T(8,128)(2,1)}, u32[]{:S(2)}) copy-start(bf16[128,5120]{1,0:T(8,128)(2,1)} %param.11) | copy-start | bytes 3932164
  17.2 108.4 %reduce-scatter.6.cloned.1.call-start = ((), (), s32[]{:S(2)}) async-start(), calls=%async_computation.5 | async-start | bytes 2359296 | tf_op jit(solution)/shard_map/reduce_scatter | solution.py:51
  42.5 3.2 copy-start.2
  75.4 3.2 copy-start.1
  86.7 2.0 copy-start.3
  91.0 94.1 %reduce-scatter.10.cloned.1.call-start = ((), (), s32[]{:S(2)}) async-start(), calls=%async_computation.7 | async-start | bytes 5898240
  125.6 3.5 copy-start.5
  129.1 3.5 copy-start.4
  144.0 1.6 copy-start.6
  144.0 274.3 %reduce-scatter.8.cloned.1.call-start = ((), (), s32[]{:S(2)}) async-start(), calls=%async_computation.6 | async-start | bytes 5406720 | tf_op jit(solution)/shard_map/reduce_scatter | solution.py:74
  145.6 5.5 %copy-start.8 = (bf16[5120,128]{1,0:T(8,128)(2,1)S(1)}, bf16[5120,128]{1,0:T(8,128)(2,1)}, u32[]{:S(2)}) copy-start(bf16[5120,128]{1,0:T(8,128)(2,1)} %param.10) | copy-start | bytes 3932164
Sparse Core Ops, SparseCore 0:
  12.6 27.1 all-gather.2
  42.2 25.7 all-gather.4
  91.1 34.4 reduce-scatter.5
  144.1 40.9 reduce-scatter.9
  189.5 228.8 reduce-scatter.7
where the time goes:
time: 425 us
  waiting for transfers between devices  308 us (72%)
  matrix products  68.5 us (16%)
  local copies, waits for them, and re-layouts  18.5 us (4%)
  other arithmetic  16 us (4%)
  between operations  14 us (3%)
    reduce_scatter x1, waiting for transfers between devices, local(): lax.psum_scatter((contract_cols(dquery, w_query) + contract_cols(dkey, w_...  231 us
    dot_general x6, matrix products, contract_cols(): lax.dot_general(left, right, (((1,), (1,)), ((), ())), preferred_element_...  29.4 us
    unnamed x6, waiting for transfers between devices  25.8 us
    dot_general x6, matrix products, contract_rows(): lax.dot_general(left, right, (((0,), (0,)), ((), ())), preferred_element_...  21.5 us
    all_gather x1, waiting for transfers between devices, local(): lax.all_gather(values, 'tm', axis=0, tiled=True)  20.2 us
    reduce_scatter x1, waiting for transfers between devices, local(): lax.psum_scatter(cache_terms.astype(jnp.bfloat16), 'tm', scatter_dimensio...  17.6 us
    unnamed x24, local copies, waits for them, and re-layouts  16.5 us
    all_gather x1, waiting for transfers between devices, local(): lax.all_gather(keys, 'tm', axis=0, tiled=True)  13.5 us
  transfers between devices with their start and end apart: 5, of which 5 were waited for; matrix products, arithmetic and copies ran while one was open for 13% of the time, Pallas kernels for 0%

commit v1 on v0

--- a/solution.py
+++ b/solution.py
@@ -27,9 +27,13 @@
     values = jnp.dot(tokens, w_value, preferred_element_type=jnp.float32).astype(jnp.bfloat16)
     d_attn = contract_cols(out_grad, w_out).astype(jnp.bfloat16)
     my_list = lax.dynamic_slice_in_dim(frame_lists, mine, 1, 0)[0]
+    compute_things = lambda vec, axis_key: jnp.concatenate(
+        lax.all_to_all(jnp.stack([vec for _ in range(lax.axis_size(axis_key))]), axis_key, 0, 0),
+        axis=0,
+    )
     key_all, value_all = (
         lax.all_gather(keys, "tm", axis=0, tiled=True),
-        lax.all_gather(values, "tm", axis=0, tiled=True),
+        compute_things(values, "tm"),
     )
     order = jnp.arange(groups, dtype=jnp.int32)
     allowed = (order == mine) | (my_list == 1) & (order < mine)

time: 425 us -> 408 us (0.960)
  waiting for transfers between devices: 308 us -> 284 us
  starting transfers between devices: 0.39 us -> 6 us
    all_gather x1 -> x0, waiting for transfers between devices: 20.2 us -> none  [local(): lax.all_gather(values, 'tm', axis=0, tiled=True)]
    all_to_all x0 -> x1, starting transfers between devices: none -> 5.65 us  [local(): lax.all_to_all(jnp.stack([vec for _ in range(lax.axis_size(axis_key))]),...]
    unnamed x24 -> x28, local copies, waits for them, and re-layouts: 16.5 us -> 15.5 us
    unnamed x6 -> x5, waiting for transfers between devices: 25.8 us -> 25.8 us
  transfers between devices with their start and end apart: 5 -> 5, of which waited for: 5 -> 4; matrix products, arithmetic and copies ran while one was open for 13% -> 13% of each run, Pallas kernels for 0% -> 0%
where the time goes in v1:
time: 408 us; the launch traced here: 407 us
  waiting for transfers between devices  284 us (70%)
  matrix products  69 us (17%)
  local copies, waits for them, and re-layouts  18.6 us (5%)
  other arithmetic  16 us (4%)
  between operations  14 us (3%)
  starting transfers between devices  6 us (1%)
    reduce_scatter x1, waiting for transfers between devices, local(): lax.psum_scatter((contract_cols(dquery, w_query) + contract_cols(dkey, w_...  230 us
    dot_general x6, matrix products, contract_cols(): lax.dot_general(left, right, (((1,), (1,)), ((), ())), preferred_element_...  29.5 us
    unnamed x5, waiting for transfers between devices  25.8 us
    dot_general x6, matrix products, contract_rows(): lax.dot_general(left, right, (((0,), (0,)), ((), ())), preferred_element_...  22.5 us
    reduce_scatter x1, waiting for transfers between devices, local(): lax.psum_scatter(cache_terms.astype(jnp.bfloat16), 'tm', scatter_dimensio...  16.9 us
    unnamed x28, local copies, waits for them, and re-layouts  15.5 us
    all_gather x1, waiting for transfers between devices, local(): lax.all_gather(keys, 'tm', axis=0, tiled=True)  10.6 us
  transfers between devices with their start and end apart: 5, of which 4 were waited for; matrix products, arithmetic and copies ran while one was open for 13% of the time, Pallas kernels for 0%

profile of v1, /device:TPU:8, one launch (start us, length us, event | category | flops | bytes accessed | tf_op | source)
XLA Modules:
  0.0 407.3 jit_solution(5775423381515940925)
XLA Ops:
  7.2 5.2 %convolution_convert_fusion.9 = bf16[512,128]{1,0:T(8,128)(2,1)} fusion(bf16[512,5120]{1,0:T(8,128)(2,1)} %param.7, bf16[5120,128]{1,0:T(8,128)(2,1)} %param.9), kind=kOutput, calls=%fused_computation.26 | convolution fusion | flops 671154176 | bytes 6684672 | tf_op jit(solution)/shard_map/dot_general | solution.py:26
  12.5 4.0 convolution_convert_fusion.7
  17.7 5.7 %all-to-all-start = ((bf16[8,512,128]{2,1,0:T(8,128)(2,1)}), bf16[8,512,128]{2,1,0:T(8,128)(2,1)S(1)}, u32[]{:S(2)}, u32[]{:S(2)}) async-start(bf16[8,512,128]{2,1,0:T(8,128)(2,1)} %stack.2), calls=%async_computation | async-start | bytes 2097152 | tf_op jit(solution)/shard_map/all_to_all | solution.py:31
  24.2 4.0 convolution_convert_fusion.10
  28.3 4.0 convolution_convert_fusion.8
  32.3 10.6 %all-gather.2.cloned.1.call-done = bf16[4096,128]{1,0:T(8,128)(2,1)} async-done(((bf16[512,128]{1,0:T(8,128)(2,1)}), bf16[4096,128]{1,0:T(8,128)(2,1)}) %all-gather.2.cloned.1.call-update) | async-done | bytes 1048592 | tf_op jit(solution)/shard_map/all_gather | solution.py:35
  42.9 2.7 fusion
  45.6 3.2 copy-done.2
  48.8 2.2 fusion.2
  51.0 7.5 %multiply_reduce_fusion = (f32[512]{0:T(512)S(1)}, f32[512,4096]{1,0:T(8,128)S(1)}, f32[512,4096]{1,0:T(8,128)}) fusion(f32[512]{0:T(512)S(1)} %fusion.2, f32[512]{0:T(512)S(1)} %get-tuple-element.21, f32[512,4096]{1,0:T(8,128)} %copy-done.2, pred[4096]{0:T(1024)(128)(4,1)S(1)} %bitcast.50, bf16[512,128]{1,0:T(8,128)(2,1)S(1)} %convolution_convert_fusion.8, ...), kind=kOutput, calls=%fused_computation.2 | convolution fusion | flops 549453312 | bytes 26355712 | tf_op jit(solution)/shard_map/dot_general | solution.py:14
  61.8 8.0 %multiply_convert_fusion = bf16[512,4096]{1,0:T(8,128)(2,1)S(1)} fusion(f32[512,4096]{1,0:T(8,128)} %copy-done.1, f32[512,4096]{1,0:T(8,128)} %get-tuple-element.23, f32[512]{0:T(512)S(1)} %get-tuple-element.15), kind=kLoop, calls=%fused_computation.1 | loop fusion | flops 8388608 | bytes 20973568 | tf_op jit(solution)/shard_map/convert_element_type | solution.py:50
  69.8 2.0 copy-done.3
  74.3 3.7 convolution_convert_fusion.6
  78.1 3.4 fusion.3
  81.5 9.7 %fusion.6 = bf16[5120,128]{0,1:T(8,128)(2,1)} fusion(bf16[512,5120]{1,0:T(8,128)(2,1)} %param.12, bf16[4096,128]{1,0:T(8,128)(2,1)} %bitcast.46, f32[512,4096]{1,0:T(8,128)} %copy-done.1), kind=kOutput, calls=%fused_computation.15 | convolution fusion | flops 1210777600 | bytes 15990784 | tf_op jit(solution)/shard_map/dot_general | solution.py:8
  91.2 16.9 %reduce-scatter.6.cloned.1.call-done = bf16[512,256]{0,1:T(8,128)(2,1)} async-done(((bf16[4096,256]{0,1:T(8,128)(2,1)}), bf16[512,256]{0,1:T(8,128)(2,1)}) %reduce-scatter.6.cloned.1.call-update) | async-done | bytes 262160 | tf_op jit(solution)/shard_map/reduce_scatter | solution.py:55
  108.1 3.4 fusion.4
  111.6 3.4 fusion.5
  115.1 3.5 pad_maximum_fusion
  118.6 7.9 %copy.18 = bf16[5120,512]{1,0:T(8,128)(2,1)} copy(bf16[5120,512]{0,1:T(8,128)(2,1)} %pad_maximum_fusion) | data formatting | bytes 10485760
  128.2 5.5 %fusion.18 = f32[512,5120]{1,0:T(8,128)} fusion(bf16[5120,128]{1,0:T(8,128)(2,1)S(1)} %copy-done.7, bf16[512,256]{0,1:T(8,128)(2,1)S(1)} %copy-done.6), kind=kOutput, calls=%fused_computation.32 | convolution fusion | flops 671088640 | bytes 11927552 | tf_op jit(solution)/shard_map/dot_general | solution.py:14
  133.7 8.2 %add_convert_fusion = bf16[512,5120]{1,0:T(8,128)(2,1)} fusion(f32[512,5120]{1,0:T(8,128)S(1)} %fusion.23, f32[512,5120]{1,0:T(8,128)} %fusion.18, bf16[5120,128]{1,0:T(8,128)(2,1)S(1)} %copy-done.9, bf16[512,256]{0,1:T(8,128)(2,1)S(1)} %copy-done.6), kind=kOutput, calls=%fused_computation | convolution fusion | flops 678952960 | bytes 27656192 | tf_op jit(solution)/shard_map/dot_general | solution.py:14
  141.9 25.8 %reduce-scatter.10.cloned.1.call-done = bf16[640,512]{1,0:T(8,128)(2,1)} async-done(((bf16[5120,512]{1,0:T(8,128)(2,1)}), bf16[640,512]{1,0:T(8,128)(2,1)}) %reduce-scatter.10.cloned.1.call-update) | async-done | bytes 655376
  170.4 230.4 %reduce-scatter.8.cloned.1.call-done = bf16[16,5120]{1,0:T(8,128)(2,1)} async-done(((bf16[512,5120]{1,0:T(8,128)(2,1)}), bf16[16,5120]{1,0:T(8,128)(2,1)}) %reduce-scatter.8.cloned.1.call-update) | async-done | bytes 163856 | tf_op jit(solution)/shard_map/reduce_scatter | solution.py:78
  (41 shorter events, 12.3 us)
Async XLA Ops:
  7.2 17.1 %copy-start = (bf16[5120,128]{1,0:T(8,128)(2,1)S(1)}, bf16[5120,128]{1,0:T(8,128)(2,1)}, u32[]{:S(2)}) copy-start(bf16[5120,128]{1,0:T(8,128)(2,1)} %param.8) | copy-start | bytes 3932164
  7.2 5.3 %copy-start.8 = (bf16[5120,128]{1,0:T(8,128)(2,1)S(1)}, bf16[5120,128]{1,0:T(8,128)(2,1)}, u32[]{:S(2)}) copy-start(bf16[5120,128]{1,0:T(8,128)(2,1)} %param.10) | copy-start | bytes 3932164
  7.2 35.7 %all-gather.2.cloned.1.call-start = ((), (), s32[]{:S(2)}) async-start(), calls=%async_computation.4 | async-start | bytes 1179648 | tf_op jit(solution)/shard_map/all_gather | solution.py:35
  17.7 33.3 %all-to-all-start = ((bf16[8,512,128]{2,1,0:T(8,128)(2,1)}), bf16[8,512,128]{2,1,0:T(8,128)(2,1)S(1)}, u32[]{:S(2)}, u32[]{:S(2)}) async-start(bf16[8,512,128]{2,1,0:T(8,128)(2,1)} %stack.2), calls=%async_computation | async-start | bytes 2097152 | tf_op jit(solution)/shard_map/all_to_all | solution.py:31
  23.3 84.8 %reduce-scatter.6.cloned.1.call-start = ((), (), s32[]{:S(2)}) async-start(), calls=%async_computation.5 | async-start | bytes 2359296 | tf_op jit(solution)/shard_map/reduce_scatter | solution.py:55
  23.3 4.9 %copy-start.11 = (bf16[128,5120]{1,0:T(8,128)(2,1)S(1)}, bf16[128,5120]{1,0:T(8,128)(2,1)}, u32[]{:S(2)}) copy-start(bf16[128,5120]{1,0:T(8,128)(2,1)} %param.11) | copy-start | bytes 3932164
  32.3 18.7 %copy-start.10 = (bf16[512,128]{1,0:T(8,128)(2,1)}, bf16[512,128]{1,0:T(8,128)(2,1)S(1)}, u32[]{:S(2)}) copy-start(bf16[512,128]{1,0:T(8,128)(2,1)S(1)} %convolution_convert_fusion.8) | copy-start | bytes 393220
  45.6 3.2 copy-start.2
  51.0 7.5 %copy-start.5 = (bf16[8,512,128]{2,1,0:T(8,128)(2,1)}, bf16[8,512,128]{2,1,0:T(8,128)(2,1)S(1)}, u32[]{:S(2)}) copy-start(bf16[8,512,128]{2,1,0:T(8,128)(2,1)S(1)} %all-to-all-done) | copy-start | bytes 3145732
  58.6 3.2 copy-start.1
  69.8 2.0 copy-start.3
  74.1 93.6 %reduce-scatter.10.cloned.1.call-start = ((), (), s32[]{:S(2)}) async-start(), calls=%async_computation.7 | async-start | bytes 5898240
  108.1 3.5 copy-start.6
  111.6 3.5 copy-start.4
  126.5 1.6 copy-start.7
  126.5 274.3 %reduce-scatter.8.cloned.1.call-start = ((), (), s32[]{:S(2)}) async-start(), calls=%async_computation.6 | async-start | bytes 5406720 | tf_op jit(solution)/shard_map/reduce_scatter | solution.py:78
  128.1 5.6 %copy-start.9 = (bf16[5120,128]{1,0:T(8,128)(2,1)S(1)}, bf16[5120,128]{1,0:T(8,128)(2,1)}, u32[]{:S(2)}) copy-start(bf16[5120,128]{1,0:T(8,128)(2,1)} %param.10) | copy-start | bytes 3932164
Sparse Core Ops, SparseCore 0:
  12.6 30.2 all-gather.1
  74.2 33.8 reduce-scatter.5
  126.7 40.9 reduce-scatter.9
  172.0 228.7 reduce-scatter.7
